TPU v7x, 32 devices: a whole 2x2x4 slice. The times are simulated.
32 devices in a mesh: groups: 2 (over y), node: 4 (over z), rep: 4 (over x, core).
Axes of the slice: x: 2, y: 2, z: 4, core: 2. Of those that a mesh axis runs over, the one named last changes fastest.
Arguments:
- node_states: bfloat16 [8, 512, 512], P(('groups', 'rep'), 'node'), parts along dimension 0, may hold values from -6 to 6
- cotangent: bfloat16 [8, 512, 512], P(('groups', 'rep'), 'node'), parts along dimension 0, may hold values from -1.1953125 to 1.1953125
- reach_blocks: int32 [8, 8, 8], P(('groups', 'rep'), 'node'), parts along dimension 0, may hold values from 0 to 7, as said below
- reach_count: int32 [8, 8], P(('groups', 'rep'), 'node'), parts along dimension 0, may hold values from 1 to 8, as said below
- level_start: int32 [8, 17], P(('groups', 'rep')), parts along dimension 0, may hold values from 0 to 512, as said below
- query_weight: bfloat16 [512, 256], replicated, may hold values from -0.25 to 0.25
- key_weight: bfloat16 [512, 256], replicated, may hold values from -0.25 to 0.25
- value_weight: bfloat16 [512, 256], replicated, may hold values from -0.25 to 0.25
- out_weight: bfloat16 [256, 512], replicated, may hold values from -0.375 to 0.375
- bias_table: float32 [4, 32], replicated, may hold values from -4 to 412
Outputs:
- updated: bfloat16 [8, 512, 512], P(('groups', 'rep'), 'node'), parts along dimension 0
- node_state_gradient: bfloat16 [8, 512, 512], P(('groups', 'rep'), 'node'), parts along dimension 0
- grad_query: float32 [1024, 256], P('groups'), parts along dimension 0
- grad_key: float32 [1024, 256], P('groups'), parts along dimension 0
- grad_value: float32 [1024, 256], P('groups'), parts along dimension 0
- grad_out: float32 [512, 512], P('groups'), parts along dimension 0
There are 2 independent parts, one for each index of `groups`. A program takes and returns all parts, laid end to end along the dimension named above; an argument that names none is the same for every part. Nothing has to cross between parts.
Inputs may be any that keep to these rules, and one draw needn't show every extreme that they name: `reach_blocks`: in row b of a graph, entry 0 is b, entries 1 to min(b, 7) are distinct blocks below b, and any later entries are b. `reach_count`: row b holds at most b + 1; row 7 of every graph holds 8. `level_start`: strictly increasing; entry 0 is 0 and entry 16 is 512.
All inputs are finite; a program needn't handle non-finite values.
Results may differ from a plain program's by a relative error of at most 0.011.
Values may be sent and summed in bfloat16 or wider, within the bound.
No kernel may reach another device: no remote copies, remote signals or barrier semaphores. Data moves between devices by JAX's collectives and lax.ppermute only.
A program may use at most 64 MiB of HBM per device.

v0:
```python
import jax
import jax.numpy as jnp
from jax import lax
from jax.sharding import PartitionSpec as P

HEADS = 4
HEAD = 64
BLOCK = 64
DIST = 32
EPS = 1e-05
NEG = -1e30
HIGH = lax.Precision.HIGHEST
CONTRACT_ROWS = (((0,), (0,)), ((), ()))
CONTRACT_COLS = (((1,), (1,)), ((), ()))


def rows_product(left, right):
    return lax.dot_general(left, right, CONTRACT_ROWS, preferred_element_type=jnp.float32)


def cols_product(left, right):
    return lax.dot_general(left, right, CONTRACT_COLS, preferred_element_type=jnp.float32)


def expand(listed):
    return jnp.repeat(jnp.repeat(listed, BLOCK, axis=0), BLOCK, axis=1)


def level_tables(starts, total, bias_table):
    level_count = starts.shape[0] - 1
    places = jnp.arange(total, dtype=jnp.int32)
    inner = starts[1:level_count]
    levels = jnp.sum((places[:, None] >= inner[None, :]).astype(jnp.int32), axis=1)
    marks = jnp.arange(level_count, dtype=jnp.int32)
    onehot = (levels[:, None] == marks[None, :]).astype(jnp.float32)
    spread = jnp.clip(marks[:, None] - marks[None, :], 0, DIST - 1)
    picks = (spread[:, :, None] == jnp.arange(DIST, dtype=jnp.int32)[None, None, :]).astype(
        jnp.float32
    )
    level_bias = jnp.einsum("hd,abd->hab", bias_table, picks, precision=HIGH)
    return (levels, onehot, level_bias)


def bias_block(row_onehot, head_bias, col_onehot):
    row_part = jnp.dot(row_onehot, head_bias, precision=HIGH)
    return lax.dot_general(row_part, col_onehot, CONTRACT_COLS, precision=HIGH)


def on_device(
    node_states,
    cotangent,
    reach_blocks,
    reach_count,
    level_start,
    query_weight,
    key_weight,
    value_weight,
    out_weight,
    bias_table,
):
    states = node_states[0]
    grads_in = cotangent[0]
    blocks = reach_blocks[0]
    counts = reach_count[0]
    starts = level_start[0]
    rows_dev = states.shape[0]
    width = query_weight.shape[1]
    total = rows_dev * lax.axis_size("node")
    offset = lax.axis_index("node") * rows_dev
    scale = HEAD ** (-0.5)
    key_blocks = total // BLOCK
    states_single_float = states.astype(jnp.float32)
    inverse_norm_scale = lax.rsqrt(
        jnp.mean(states_single_float * states_single_float, axis=1, keepdims=True) + EPS
    )
    centered_states = states_single_float * inverse_norm_scale
    normalized_states = centered_states.astype(jnp.bfloat16)
    queries = jnp.dot(normalized_states, query_weight, preferred_element_type=jnp.float32).astype(
        jnp.bfloat16
    )
    keys = jnp.dot(normalized_states, key_weight, preferred_element_type=jnp.float32).astype(
        jnp.bfloat16
    )
    values = jnp.dot(normalized_states, value_weight, preferred_element_type=jnp.float32).astype(
        jnp.bfloat16
    )
    keys_all, values_all = (
        lax.all_gather(keys, "node", axis=0, tiled=True),
        lax.all_gather(values, "node", axis=0, tiled=True),
    )
    levels, onehot, level_bias = level_tables(starts, total, bias_table)
    positions = jnp.arange(total, dtype=jnp.int32)
    local = jnp.arange(rows_dev, dtype=jnp.int32)
    row_ids = offset + local
    row_levels = lax.dynamic_slice_in_dim(levels, offset, rows_dev, 0)
    row_onehot = lax.dynamic_slice_in_dim(onehot, offset, rows_dev, 0)
    slots = jnp.arange(blocks.shape[1], dtype=jnp.int32)
    live = slots[None, :] < counts[:, None]
    kinds = jnp.arange(key_blocks, dtype=jnp.int32)
    listed = jnp.any((blocks[:, :, None] == kinds[None, None, :]) & live[:, :, None], axis=1)
    visible = expand(listed) & (
        (levels[None, :] < row_levels[:, None]) | (positions[None, :] == row_ids[:, None])
    )
    prob_list = []
    lse_list = []
    mixed_list = []
    for head in range(HEADS):
        lower = head * HEAD
        scores = (
            cols_product(queries[:, lower : lower + HEAD], keys_all[:, lower : lower + HEAD])
            * scale
        )
        scores = scores + bias_block(row_onehot, level_bias[head], onehot)
        scores = jnp.where(visible, scores, NEG)
        peak = jnp.max(scores, axis=1, keepdims=True)
        mass = jnp.sum(jnp.where(visible, jnp.exp(scores - peak), 0.0), axis=1, keepdims=True)
        lse = peak + jnp.log(mass)
        probs = jnp.where(visible, jnp.exp(scores - lse), 0.0).astype(jnp.bfloat16)
        prob_list.append(probs)
        lse_list.append(lse)
        mixed_list.append(
            jnp.dot(probs, values_all[:, lower : lower + HEAD], preferred_element_type=jnp.float32)
        )
    mixed = jnp.concatenate(mixed_list, axis=1).astype(jnp.bfloat16)
    updated = (
        states_single_float + jnp.dot(mixed, out_weight, preferred_element_type=jnp.float32)
    ).astype(jnp.bfloat16)
    partial_out = rows_product(mixed, grads_in)
    d_mixed = cols_product(grads_in, out_weight).astype(jnp.bfloat16)
    score_grads = []
    delta_list = []
    query_grads = []
    for head in range(HEADS):
        lower = head * HEAD
        mixed_head = d_mixed[:, lower : lower + HEAD]
        delta = jnp.sum(
            mixed_head.astype(jnp.float32) * mixed[:, lower : lower + HEAD].astype(jnp.float32),
            axis=1,
            keepdims=True,
        )
        d_probs = cols_product(mixed_head, values_all[:, lower : lower + HEAD])
        d_scores = (prob_list[head].astype(jnp.float32) * (d_probs - delta)).astype(jnp.bfloat16)
        score_grads.append(d_scores)
        delta_list.append(delta)
        query_grads.append(
            jnp.dot(d_scores, keys_all[:, lower : lower + HEAD], preferred_element_type=jnp.float32)
            * scale
        )
    d_queries = jnp.concatenate(query_grads, axis=1).astype(jnp.bfloat16)
    key_pieces = []
    value_pieces = []
    for head in range(HEADS):
        lower = head * HEAD
        score_part = score_grads[head]
        prob_part = prob_list[head]
        key_pieces.append(rows_product(score_part, queries[:, lower : lower + HEAD]) * scale)
        value_pieces.append(rows_product(prob_part, d_mixed[:, lower : lower + HEAD]))
    key_value_grads = lax.psum_scatter(
        jnp.concatenate(key_pieces + value_pieces, axis=1).astype(jnp.bfloat16),
        "node",
        scatter_dimension=0,
        tiled=True,
    ).astype(jnp.float32)
    d_keys = key_value_grads[:, :width].astype(jnp.bfloat16)
    d_values = key_value_grads[:, width:].astype(jnp.bfloat16)
    normalized_gradient = (
        cols_product(d_queries, query_weight)
        + cols_product(d_keys, key_weight)
        + cols_product(d_values, value_weight)
    )
    node_state_gradient = (
        grads_in.astype(jnp.float32)
        + inverse_norm_scale
        * (
            normalized_gradient
            - centered_states
            * jnp.mean(normalized_gradient * centered_states, axis=1, keepdims=True)
        )
    ).astype(jnp.bfloat16)
    partial_query = rows_product(normalized_states, d_queries)
    partial_key = rows_product(normalized_states, d_keys)
    partial_value = rows_product(normalized_states, d_values)
    total_query, total_key, total_value, total_out = lax.psum(
        (partial_query, partial_key, partial_value, partial_out), ("node", "rep")
    )
    return (
        updated[None],
        node_state_gradient[None],
        total_query,
        total_key,
        total_value,
        total_out,
    )


def solution(mesh):
    in_specs = (
        P(("groups", "rep"), "node", None),
        P(("groups", "rep"), "node", None),
        P(("groups", "rep"), "node", None),
        P(("groups", "rep"), "node"),
        P(("groups", "rep"), None),
        P(),
        P(),
        P(),
        P(),
        P(),
    )
    out_specs = (
        P(("groups", "rep"), "node", None),
        P(("groups", "rep"), "node", None),
        P("groups", None),
        P("groups", None),
        P("groups", None),
        P("groups", None),
    )
    return jax.shard_map(
        on_device, mesh=mesh, in_specs=in_specs, out_specs=out_specs, check_vma=False
    )
```

profile of v0, /device:TPU:0, one launch (start us, length us, event | category | flops | bytes accessed | tf_op | source)
XLA Modules:
  0.0 189.7 jit_solution(12456625626089858018)
XLA Ops:
  7.3 0.6 copy-done.12
  8.0 0.7 copy-done.10
  8.9 0.6 copy-done.13
  9.5 1.0 fusion.42
  11.0 0.6 copy-done.11
  11.6 0.6 convolution_bitcast_fusion
  13.4 0.3 convolution_convert_fusion.3
  13.6 0.3 copy-done.5
  14.1 0.2 convolution_convert_fusion.1
  14.4 15.6 %all_gather.7 = bf16[512,256]{1,0:T(8,128)(2,1)S(1)} all-gather(bf16[128,256]{1,0:T(8,128)(2,1)S(1)} %convolution_convert_fusion.1), channel_id=1, replica_groups=mesh['groups'=2,'node'=4,'rep'=4] {'node'}, dimensions={0}, use_global_device_ids=true | all-gather | bytes 327680 | tf_op jit(solution)/shard_map/all_gather | solution.py:89
  30.0 14.6 %all_gather.6 = bf16[512,256]{1,0:T(8,128)(2,1)S(1)} all-gather(bf16[128,256]{1,0:T(8,128)(2,1)S(1)} %convolution_convert_fusion.2), channel_id=1, replica_groups=mesh['groups'=2,'node'=4,'rep'=4] {'node'}, dimensions={0}, use_global_device_ids=true | all-gather | bytes 327680 | tf_op jit(solution)/shard_map/all_gather | solution.py:88
  44.6 0.4 fusion.46
  45.0 0.4 fusion.43
  45.4 0.3 fusion.124
  45.7 0.4 fusion.127
  46.0 0.4 fusion.44
  46.4 0.3 fusion.126
  46.7 0.4 fusion.45
  47.1 0.4 fusion.125
  47.5 0.4 select_reduce_fusion.3
  47.9 0.3 select_convert_fusion.3
  48.2 0.3 convolution_convert_fusion.10
  48.7 0.3 convolution_convert_fusion.8
  49.0 0.4 copy-done.3
  49.9 0.2 multiply_reduce_fusion.3
  50.3 0.3 fusion.14
  50.8 0.3 fusion.16
  51.3 0.3 fusion.21
  51.8 0.3 fusion.25
  52.7 1.0 copy.27
  54.0 0.3 fusion.31
  54.3 0.3 fusion.33
  54.8 0.2 fusion.105
  55.0 1.0 fusion.50
  56.0 1.1 fusion.104
  57.1 19.4 %reduce-scatter.4.cloned.1.call-done = bf16[128,512]{1,0:T(8,128)(2,1)} async-done(((bf16[512,512]{1,0:T(8,128)(2,1)}), bf16[128,512]{1,0:T(8,128)(2,1)}) %reduce-scatter.4.cloned.1.call-update) | async-done | bytes 131088
  76.5 2.0 %fusion.78 = f32[512,256]{1,0:T(8,128)} fusion(bf16[128,512]{1,0:T(8,128)(2,1)} %reduce-scatter.4.cloned.1.call-done, bf16[1,128,512]{2,1,0:T(8,128)(2,1)S(1)} %copy-done.1, f32[128]{0:T(128)S(1)} %add_rsqrt_fusion), kind=kOutput, calls=%fused_computation.125 | convolution fusion | flops 33751040 | bytes 721408 | tf_op jit(solution)/shard_map/dot_general | solution.py:18
  78.5 1.1 fusion.75
  79.6 0.9 fusion.17
  80.7 0.3 fusion.37
  81.1 0.8 fusion.49
  81.9 95.8 %all-reduce.3.cloned.1.call-done = (f32[512,256]{1,0:T(8,128)}, f32[512,256]{1,0:T(8,128)}, f32[512,256]{1,0:T(8,128)}, f32[256,512]{1,0:T(8,128)}) async-done(((f32[512,256]{1,0:T(8,128)}, f32[512,256]{1,0:T(8,128)}, f32[512,256]{1,0:T(8,128)}, f32[256,512]{1,0:T(8,128)}), (f32[512,256]{1,0:T(8,128)}, f32[512,256]{1,0:T(8,128)}, f32[512,256]{1,0:T(8,128)}, ...) | async-done | bytes 2097168 | tf_op jit(solution)/shard_map/psum | solution.py:183
  177.7 1.9 %copy.53 = f32[512,256]{1,0:T(8,128)} copy(f32[512,256]{1,0:T(8,128)} %get-tuple-element.43) | data formatting | bytes 1048576
  179.6 0.8 copy.54
  180.4 0.4 copy-done.7
  180.8 0.8 copy.55
  181.6 0.4 copy-done.6
  182.0 0.8 copy.56
  (60 shorter events, 5.0 us)
Async XLA Ops:
  7.2 7.0 %copy-start = (bf16[512,256]{1,0:T(8,128)(2,1)S(1)}, bf16[512,256]{1,0:T(8,128)(2,1)}, u32[]{:S(2)}) copy-start(bf16[512,256]{1,0:T(8,128)(2,1)} %param.17) | copy-start | bytes 786436
  7.2 69.3 %reduce-scatter.4.cloned.1.call-start = ((), (), s32[]{:S(2)}) async-start(), calls=%async_computation.1 | async-start | bytes 655360
  7.3 0.7 copy-start.12
  8.0 0.7 copy-start.10
  8.8 0.7 copy-start.13
  10.9 0.7 copy-start.11
  11.6 1.7 copy-start.4
  12.3 1.0 copy-start.1
  12.9 1.0 copy-start.5
  48.5 1.0 copy-start.3
  48.7 0.9 copy-start.2
  53.7 123.9 %all-reduce.3.cloned.1.call-start = ((), (), s32[]{:S(2)}) async-start(), calls=%async_computation.2 | async-start | bytes 4194304 | tf_op jit(solution)/shard_map/psum | solution.py:183
  76.5 2.0 %copy-start.9 = (bf16[128,512]{1,0:T(8,128)(2,1)S(1)}, bf16[128,512]{1,0:T(8,128)(2,1)}, u32[]{:S(2)}) copy-start(bf16[128,512]{1,0:T(8,128)(2,1)} %reduce-scatter.4.cloned.1.call-done) | copy-start | bytes 393220
  177.6 1.9 %copy-start.8 = (f32[512,256]{1,0:T(8,128)S(1)}, f32[512,256]{1,0:T(8,128)}, u32[]{:S(2)}) copy-start(f32[512,256]{1,0:T(8,128)} %get-tuple-element.44) | copy-start | bytes 1572868
  179.6 1.2 copy-start.7
  180.8 1.2 copy-start.6
Sparse Core Ops, SparseCore 0:
  53.8 22.5 reduce-scatter.3
  81.0 96.5 all-reduce.2
where the time goes:
time: 190 us
  waiting for transfers between devices  115 us (61%)
  blocking collectives  30.2 us (16%)
  matrix products  16.7 us (9%)
  between operations  14.3 us (8%)
  local copies, waits for them, and re-layouts  10.3 us (5%)
  other arithmetic  2.95 us (2%)
    psum x1, waiting for transfers between devices, on_device(): lax.psum((partial_query, partial_key, partial_value, partial_out), ('node...  95.8 us
    unnamed x3, waiting for transfers between devices  19.4 us
    all_gather x1, blocking collectives, on_device(): lax.all_gather(values, 'node', axis=0, tiled=True)  15.6 us
    all_gather x1, blocking collectives, on_device(): lax.all_gather(keys, 'node', axis=0, tiled=True)  14.6 us
    unnamed x33, local copies, waits for them, and re-layouts  9.64 us
    dot_general x12, matrix products, rows_product(): lax.dot_general(left, right, CONTRACT_ROWS, preferred_element_type=jnp.fl...  6.81 us
  transfers between devices with their start and end apart: 2, of which 2 were waited for; matrix products, arithmetic and copies ran while one was open for 3% of the time, Pallas kernels for 0%

commit v1 on v0

--- a/solution.py
+++ b/solution.py
@@ -58,6 +58,25 @@
     out_weight,
     bias_table,
 ):
+
+    def register_arrays(s0, axis_id, axis_k=0):
+        current_block = lax.axis_size(axis_id)
+        small, carry, m_next = (current_block, lax.axis_index(axis_id), s0.shape[axis_k])
+        y, found_now = (s0, 1)
+        while found_now < small:
+            y = jnp.concatenate(
+                [
+                    y,
+                    lax.ppermute(
+                        y, axis_id, [(ix, (ix - found_now) % small) for ix in range(small)]
+                    ),
+                ],
+                axis=axis_k,
+            )
+            found_now = 2 * found_now
+        shaped = jnp.roll(y, carry * m_next, axis=axis_k)
+        return shaped
+
     states = node_states[0]
     grads_in = cotangent[0]
     blocks = reach_blocks[0]
@@ -85,7 +104,7 @@
         jnp.bfloat16
     )
     keys_all, values_all = (
-        lax.all_gather(keys, "node", axis=0, tiled=True),
+        register_arrays(keys, "node"),
         lax.all_gather(values, "node", axis=0, tiled=True),
     )
     levels, onehot, level_bias = level_tables(starts, total, bias_table)

time: 190 us -> 183 us (0.963)
  blocking collectives: 30.2 us -> 16 us
  starting transfers between devices: 0.08 us -> 5.18 us
  waiting for transfers between devices: 115 us -> 112 us
  local copies, waits for them, and re-layouts: 10.3 us -> 12.5 us
    all_gather x1 -> x0, blocking collectives: 14.6 us -> none  [on_device(): lax.all_gather(keys, 'node', axis=0, tiled=True)]
    ppermute x0 -> x2, starting transfers between devices: none -> 5.1 us  [register_arrays(): lax.ppermute(y, axis_id, [(ix, (ix - found_now) % small) for ix in range(...]
    unnamed x3, waiting for transfers between devices: 19.4 us -> 16.3 us
    unnamed x33 -> x55, local copies, waits for them, and re-layouts: 9.64 us -> 11 us
  transfers between devices with their start and end apart: 2 -> 4, of which waited for: 2 -> 2; matrix products, arithmetic and copies ran while one was open for 3% -> 5% of each run, Pallas kernels for 0% -> 0%
where the time goes in v1:
time: 183 us; the launch traced here: 182 us
  waiting for transfers between devices  112 us (61%)
  matrix products  18.5 us (10%)
  blocking collectives  16 us (9%)
  between operations  14.5 us (8%)
  local copies, waits for them, and re-layouts  12.5 us (7%)
  starting transfers between devices  5.18 us (3%)
  other arithmetic  3.66 us (2%)
    psum x1, waiting for transfers between devices, on_device(): lax.psum((partial_query, partial_key, partial_value, partial_out), ('node...  95.7 us
    unnamed x3, waiting for transfers between devices  16.3 us
    all_gather x1, blocking collectives, on_device(): lax.all_gather(values, 'node', axis=0, tiled=True)  16 us
    unnamed x55, local copies, waits for them, and re-layouts  11 us
    dot_general x12, matrix products, rows_product(): lax.dot_general(left, right, CONTRACT_ROWS, preferred_element_type=jnp.fl...  6.82 us
    ppermute x2, starting transfers between devices, register_arrays(): lax.ppermute(y, axis_id, [(ix, (ix - found_now) % small) for ix in range(...  5.1 us
  transfers between devices with their start and end apart: 4, of which 2 were waited for; matrix products, arithmetic and copies ran while one was open for 5% of the time, Pallas kernels for 0%

profile of v1, /device:TPU:0, one launch (start us, length us, event | category | flops | bytes accessed | tf_op | source)
XLA Modules:
  0.0 182.3 jit_solution(12391006468084200230)
XLA Ops:
  7.2 1.1 fusion.42
  8.6 5.1 %collective-permute-start = (bf16[128,256]{1,0:T(8,128)(2,1)S(1)}, bf16[128,256]{1,0:T(8,128)(2,1)S(1)}, u32[]{:S(2)}, u32[]{:S(2)}) collective-permute-start(bf16[128,256]{1,0:T(8,128)(2,1)S(1)} %get-tuple-element.27), channel_id=1, source_target_pairs={{0,12},{4,0},{8,4},{12,8},{1,13},{5,1},{9,5},{13,9},{2,14},{6,2},{... | collective-permute-start | bytes 196616 | tf_op jit(solution)/shard_map/ppermute | solution.py:70
  13.7 0.7 copy-done.21
  14.4 0.6 copy-done.22
  15.2 0.5 copy-done.20
  15.7 0.6 convolution_bitcast_fusion
  17.9 0.4 fusion.46
  18.3 0.4 fusion.43
  18.7 0.4 fusion.44
  19.2 0.4 fusion.45
  19.6 0.7 copy-done.19
  20.6 0.7 pad_maximum_fusion
  21.3 16.0 %all_gather.3 = bf16[512,256]{1,0:T(8,128)(2,1)S(1)} all-gather(bf16[128,256]{1,0:T(8,128)(2,1)S(1)} %convolution_convert_fusion.1), channel_id=1, replica_groups=mesh['groups'=2,'node'=4,'rep'=4] {'node'}, dimensions={0}, use_global_device_ids=true | all-gather | bytes 327680 | tf_op jit(solution)/shard_map/all_gather | solution.py:108
  37.8 0.9 constant_dynamic-update-slice_fusion.3
  38.8 0.9 constant_dynamic-update-slice_fusion
  39.7 0.3 fusion.126
  40.0 0.3 fusion.128
  40.2 0.4 fusion.127
  40.6 0.4 fusion.129
  41.0 0.4 select_reduce_fusion.3
  41.4 0.3 select_convert_fusion.3
  41.7 0.3 convolution_convert_fusion.10
  42.2 0.3 convolution_convert_fusion.8
  42.5 0.3 copy-done.10
  42.8 0.8 multiply_reduce_fusion.3
  43.9 0.8 fusion.30
  45.2 0.9 fusion.31
  46.6 0.3 fusion.21
  47.1 0.3 fusion.25
  48.0 1.0 copy.27
  49.0 0.3 fusion.33
  49.6 0.5 copy-done.14
  50.3 0.5 copy-done.11
  50.8 1.0 fusion.50
  51.8 1.1 fusion.104
  52.9 16.2 %reduce-scatter.4.cloned.1.call-done = bf16[128,512]{1,0:T(8,128)(2,1)} async-done(((bf16[512,512]{1,0:T(8,128)(2,1)}), bf16[128,512]{1,0:T(8,128)(2,1)}) %reduce-scatter.4.cloned.1.call-update) | async-done | bytes 131088
  69.2 2.0 %fusion.78 = f32[512,256]{1,0:T(8,128)} fusion(bf16[128,512]{1,0:T(8,128)(2,1)} %reduce-scatter.4.cloned.1.call-done, bf16[1,128,512]{2,1,0:T(8,128)(2,1)S(1)} %copy-done.1, f32[128]{0:T(128)S(1)} %copy-done.18), kind=kOutput, calls=%fused_computation.126 | convolution fusion | flops 33751040 | bytes 721408 | tf_op jit(solution)/shard_map/dot_general | solution.py:18
  71.2 1.1 fusion.75
  72.4 0.9 fusion.17
  73.5 0.3 fusion.37
  73.8 0.8 fusion.49
  74.6 95.7 %all-reduce.3.cloned.1.call-done = (f32[512,256]{1,0:T(8,128)}, f32[512,256]{1,0:T(8,128)}, f32[512,256]{1,0:T(8,128)}, f32[256,512]{1,0:T(8,128)}) async-done(((f32[512,256]{1,0:T(8,128)}, f32[512,256]{1,0:T(8,128)}, f32[512,256]{1,0:T(8,128)}, f32[256,512]{1,0:T(8,128)}), (f32[512,256]{1,0:T(8,128)}, f32[512,256]{1,0:T(8,128)}, f32[512,256]{1,0:T(8,128)}, ...) | async-done | bytes 2097168 | tf_op jit(solution)/shard_map/psum | solution.py:202
  170.3 1.9 %copy.58 = f32[512,256]{1,0:T(8,128)} copy(f32[512,256]{1,0:T(8,128)} %get-tuple-element.45) | data formatting | bytes 1048576
  172.2 0.8 copy.59
  173.0 0.4 copy-done.7
  173.4 0.8 copy.60
  174.2 0.4 copy-done.6
  174.7 0.8 copy.61
  (87 shorter events, 6.0 us)
Async XLA Ops:
  7.2 1.1 copy-start
  7.2 1.1 copy-start.1
  7.2 62.0 %reduce-scatter.4.cloned.1.call-start = ((), (), s32[]{:S(2)}) async-start(), calls=%async_computation.1 | async-start | bytes 655360
  8.3 9.3 %copy-start.17 = (f32[128]{0:T(128)}, f32[128]{0:T(128)S(1)}, u32[]{:S(2)}) copy-start(f32[128]{0:T(128)S(1)} %add_rsqrt_fusion) | copy-start | bytes 1540
  8.3 8.0 %copy-start.5 = (bf16[512,256]{1,0:T(8,128)(2,1)S(1)}, bf16[512,256]{1,0:T(8,128)(2,1)}, u32[]{:S(2)}) copy-start(bf16[512,256]{1,0:T(8,128)(2,1)} %param.15) | copy-start | bytes 786436
  8.6 12.0 %collective-permute-start = (bf16[128,256]{1,0:T(8,128)(2,1)S(1)}, bf16[128,256]{1,0:T(8,128)(2,1)S(1)}, u32[]{:S(2)}, u32[]{:S(2)}) collective-permute-start(bf16[128,256]{1,0:T(8,128)(2,1)S(1)} %get-tuple-element.27), channel_id=1, source_target_pairs={{0,12},{4,0},{8,4},{12,8},{1,13},{5,1},{9,5},{13,9},{2,14},{6,2},{... | collective-permute-start | bytes 196616 | tf_op jit(solution)/shard_map/ppermute | solution.py:70
  13.7 0.7 copy-start.21
  14.4 0.7 copy-start.22
  15.0 0.7 copy-start.20
  16.4 1.3 copy-start.3
  18.7 1.6 copy-start.4
  19.1 1.2 copy-start.2
  19.6 0.7 copy-start.19
  21.3 16.5 %collective-permute-start.1 = (bf16[256,256]{1,0:T(8,128)(2,1)}, bf16[256,256]{1,0:T(8,128)(2,1)}, u32[]{:S(2)}, u32[]{:S(2)}) collective-permute-start(bf16[256,256]{1,0:T(8,128)(2,1)} %pad_maximum_fusion), channel_id=1, source_target_pairs={{0,8},{4,12},{8,0},{12,4},{1,9},{5,13},{9,1},{13,5},{2,10},{6,14},... | collective-permute-start | bytes 393224 | tf_op jit(solution)/shard_map/ppermute | solution.py:70
  42.2 0.6 copy-start.10
  42.5 1.2 copy-start.12
  49.0 121.3 %all-reduce.3.cloned.1.call-start = ((), (), s32[]{:S(2)}) async-start(), calls=%async_computation.2 | async-start | bytes 4194304 | tf_op jit(solution)/shard_map/psum | solution.py:202
  49.3 0.7 copy-start.14
  49.3 0.7 copy-start.15
  50.1 0.7 copy-start.11
  50.1 0.7 copy-start.13
  50.1 0.7 copy-start.16
  50.8 1.0 copy-start.18
  69.2 2.0 %copy-start.9 = (bf16[128,512]{1,0:T(8,128)(2,1)S(1)}, bf16[128,512]{1,0:T(8,128)(2,1)}, u32[]{:S(2)}) copy-start(bf16[128,512]{1,0:T(8,128)(2,1)} %reduce-scatter.4.cloned.1.call-done) | copy-start | bytes 393220
  170.3 1.9 %copy-start.8 = (f32[512,256]{1,0:T(8,128)S(1)}, f32[512,256]{1,0:T(8,128)}, u32[]{:S(2)}) copy-start(f32[512,256]{1,0:T(8,128)} %get-tuple-element.46) | copy-start | bytes 1572868
  172.2 1.2 copy-start.7
  173.4 1.2 copy-start.6
Sparse Core Ops, SparseCore 0:
  49.1 20.0 reduce-scatter.3
  73.7 96.4 all-reduce.2
